TPU v7x, 32 devices: a whole 2x2x4 slice. The times are simulated.
32 devices in a mesh: leaf: 16 (over z, y, x), col: 2 (over core).
Axes of the slice: x: 2, y: 2, z: 4, core: 2. Of those that a mesh axis runs over, the one named last changes fastest.
Arguments:
- sources: bfloat16 [65536, 256], P('leaf', 'col'), may hold values from -6 to 6
- near_tiles: bfloat16 [256, 8, 256, 256], P('leaf', 'col'), may hold values from -0.125 to 0.125
- near_index: int32 [256, 8], P('leaf'), may hold values from 0 to 255, as said below
- near_count: int32 [256], P('leaf'), may hold values from 1 to 8, as said below
- leaf_basis: bfloat16 [256, 64, 256], P('leaf'), may hold values from -0.375 to 0.375
- leaf_coupling: bfloat16 [256, 64, 256], P('leaf'), may hold values from -0.375 to 0.375
- leaf_far: int32 [256, 4], P('leaf'), may hold values from 0 to 255, as said below
- up_leaf: bfloat16 [32, 64, 512], P('leaf'), may hold values from -0.25 to 0.25
- mid_coupling: bfloat16 [32, 64, 256], P('leaf'), may hold values from -0.375 to 0.375
- mid_far: int32 [32, 4], P('leaf'), may hold values from 0 to 31, as said below
- up_mid: bfloat16 [32, 64, 64], P('leaf'), may hold values from -0.75 to 0.75
- top_coupling: bfloat16 [4, 64, 256], replicated, may hold values from -0.4375 to 0.4375
Outputs:
- product: float32 [65536, 256], P('leaf', 'col')
Inputs may be any that keep to these rules, and one draw needn't show every extreme that they name: `near_index`: entry 0 of row i is i; the other 7 entries are distinct leaves j with j != i and |i - j| <= 8. Only the first near_count[i] slots of leaf i count; some leaf has all 8. `leaf_far`: row i holds 4 distinct leaves j != i with |i // 8 - j // 8| <= 1. `mid_far`: row a holds 4 distinct middle clusters b != a with |a // 8 - b // 8| <= 1.
All inputs are finite; a program needn't handle non-finite values.
Results may differ from a plain program's by a relative error of at most 0.01.
Values may be sent and summed in bfloat16 or wider, within the bound.
No kernel may reach another device: no remote copies, remote signals or barrier semaphores. Data moves between devices by JAX's collectives and lax.ppermute only.
A program may use at most 128 MiB of HBM per device.

v0:
```python
import jax
import jax.numpy as jnp
from jax import lax
from jax.sharding import PartitionSpec as P

CHILD = 8
FAR = 4


def padded(x, sides, width):
    for axis, dim in sides:
        size, length = (lax.axis_size(axis), x.shape[dim])
        up = [(i, (i + 1) % size) for i in range(size - 1)]
        down = [(j, i) for i, j in up]
        last = lax.slice_in_dim(x, length - width, length, axis=dim)
        first = lax.slice_in_dim(x, 0, width, axis=dim)
        before = lax.ppermute(last, axis, up)
        after = lax.ppermute(first, axis, down)
        x = jnp.concatenate([before, x, after], axis=dim)
    return x


def shards(
    sources,
    near_tiles,
    near_index,
    near_count,
    leaf_basis,
    leaf_coupling,
    leaf_far,
    up_leaf,
    mid_coupling,
    mid_far,
    up_mid,
    top_coupling,
):
    f32 = jnp.float32
    bf16 = jnp.bfloat16
    leaf_count = leaf_basis.shape[0]
    rank_size = leaf_basis.shape[1]
    leaf_size = leaf_basis.shape[2]
    col_count = sources.shape[1]
    mid_count = leaf_count // CHILD
    total_top = top_coupling.shape[0]
    device = lax.axis_index("leaf")
    first_leaf = device * leaf_count
    first_mid = device * mid_count
    window = padded(sources, (("leaf", 0),), CHILD * leaf_size)
    near_local = near_index - (first_leaf - CHILD)
    all_tiles = lax.all_gather(near_tiles, "col", axis=1, tiled=True)
    slot_count = all_tiles.shape[1]
    blocks = window.reshape(-1, leaf_size, window.shape[1])
    picked = blocks[near_local]
    live_mask = jnp.arange(slot_count)[None, :] < near_count[:, None]
    picked = jnp.where(live_mask[:, :, None, None], picked, jnp.zeros((), bf16))
    result = jnp.einsum("lsij,lsjc->lic", all_tiles, picked, preferred_element_type=f32)
    near_part = result.reshape(leaf_count * leaf_size, window.shape[1])
    leaf_blocks = sources.reshape(leaf_count, leaf_size, col_count)
    leaf_coef = jnp.einsum(
        "lrk,lkc->lrc", leaf_basis, leaf_blocks, preferred_element_type=f32
    ).astype(bf16)
    mid_coef = jnp.einsum(
        "qrk,qkc->qrc",
        up_leaf,
        leaf_coef.reshape(mid_count, CHILD * rank_size, col_count),
        preferred_element_type=f32,
    ).astype(bf16)
    mid_lift = jnp.einsum("qrs,qsc->qrc", up_mid, mid_coef, preferred_element_type=f32).astype(bf16)
    parent = (first_mid + jnp.arange(mid_count)) // CHILD
    mid_flat = mid_far.reshape(-1)
    top_range = jnp.arange(total_top)
    coef_piece = lax.all_gather(mid_coef, "leaf", axis=0, tiled=True)
    lift_piece = lax.all_gather(mid_lift, "leaf", axis=0, tiled=True)
    global_ids = jnp.arange(coef_piece.shape[0])
    group_map = (top_range[:, None] == (global_ids // CHILD)[None, :]).astype(bf16)
    top_total = jnp.einsum("pk,krc->prc", group_map, lift_piece, preferred_element_type=f32)
    global_ids = jnp.arange(coef_piece.shape[0])
    pick_map = (mid_flat[:, None] == global_ids[None, :]).astype(bf16)
    mid_picked = jnp.einsum("ik,krc->irc", pick_map, coef_piece, preferred_element_type=f32)
    top_coef = top_total.astype(bf16)
    parent_rows = top_coupling[parent]
    keep_mask = top_range[None, :] != parent[:, None]
    stacked = jnp.where(keep_mask[:, :, None, None], top_coef[None], jnp.zeros((), bf16))
    top_field = jnp.einsum(
        "qrk,qkc->qrc",
        parent_rows,
        stacked.reshape(mid_count, total_top * rank_size, col_count),
        preferred_element_type=f32,
    ).astype(bf16)
    mid_chosen = mid_picked.astype(bf16).reshape(mid_count, FAR * rank_size, col_count)
    mid_field = (
        jnp.einsum("qrk,qkc->qrc", mid_coupling, mid_chosen, preferred_element_type=f32)
        + jnp.einsum("qrs,qrc->qsc", up_mid, top_field, preferred_element_type=f32)
    ).astype(bf16)
    leaf_window = padded(leaf_coef, (("leaf", 0),), CHILD)
    far_local = leaf_far - (first_leaf - CHILD)
    leaf_chosen = leaf_window[far_local].reshape(leaf_count, FAR * rank_size, col_count)
    down_part = jnp.einsum("qrs,qrc->qsc", up_leaf, mid_field, preferred_element_type=f32).reshape(
        leaf_count, rank_size, col_count
    )
    leaf_field = (
        jnp.einsum("lrk,lkc->lrc", leaf_coupling, leaf_chosen, preferred_element_type=f32)
        + down_part
    ).astype(bf16)
    far_part = jnp.einsum(
        "lrk,lrc->lkc", leaf_basis, leaf_field, preferred_element_type=f32
    ).reshape(leaf_count * leaf_size, col_count)
    return near_part + far_part


def solution(mesh):
    return jax.shard_map(
        shards,
        mesh=mesh,
        in_specs=(
            P("leaf", "col"),
            P("leaf", "col", None, None),
            P("leaf", None),
            P("leaf"),
            P("leaf", None, None),
            P("leaf", None, None),
            P("leaf", None),
            P("leaf", None, None),
            P("leaf", None, None),
            P("leaf", None),
            P("leaf", None, None),
            P(),
        ),
        out_specs=P("leaf", "col"),
        check_vma=False,
    )
```

profile of v0, /device:TPU:0, one launch (start us, length us, event | category | flops | bytes accessed | tf_op | source)
XLA Modules:
  0.0 168.7 jit_solution(13844385451105794318)
XLA Ops:
  6.5 0.0 copy-start
  6.5 0.0 copy-start.1
  6.5 0.0 all-gather.2.cloned.1.call-start
  6.5 0.7 all-gather.2.cloned.1.call-update
  7.3 0.0 copy-start.9
  7.3 0.0 copy-start.4
  7.3 0.0 copy-start.6
  7.3 0.0 copy-start.11
  7.3 0.0 copy-start.7
  7.3 0.0 copy-start.10
  7.3 0.0 copy-start.8
  7.3 0.0 copy-start.5
  7.3 0.2 copy-done
  7.6 0.3 copy-done.1
  7.9 0.3 convolution_convert_fusion
  8.3 4.9 %collective-permute-start.2 = (bf16[8,64,128]{2,1,0:T(8,128)(2,1)S(1)}, bf16[8,64,128]{2,1,0:T(8,128)(2,1)S(1)}, u32[]{:S(2)}, u32[]{:S(2)}) collective-permute-start(bf16[8,64,128]{2,1,0:T(8,128)(2,1)S(1)} %get-tuple-element.7), channel_id=1, source_target_pairs={{0,2},{2,4},{4,6},{6,8},{8,10},{10,12},{12,14},{14,16},{16,18},{18... | collective-permute-start | bytes 393224 | tf_op jit(solution)/shard_map/ppermute | solution.py:17
  13.2 1.3 collective-permute-start.3
  14.5 1.1 fusion.33
  15.5 5.4 %collective-permute-start = (bf16[2048,128]{1,0:T(8,128)(2,1)}, bf16[2048,128]{1,0:T(8,128)(2,1)}, u32[]{:S(2)}, u32[]{:S(2)}) collective-permute-start(bf16[2048,128]{1,0:T(8,128)(2,1)} %get-tuple-element.5), channel_id=1, source_target_pairs={{0,2},{2,4},{4,6},{6,8},{8,10},{10,12},{12,14},{14,16},{16,18},{18... | collective-permute-start | bytes 1572872 | tf_op jit(solution)/shard_map/ppermute | solution.py:17
  20.9 1.3 collective-permute-start.1
  22.2 0.0 copy-done.9
  22.2 0.1 copy.27
  22.3 0.1 reshape.160
  22.4 0.0 copy-done.4
  22.4 0.2 convolution_convert_fusion.5
  22.6 0.0 copy-done.6
  22.6 0.1 fusion.12
  22.7 0.0 copy-start.3
  22.7 57.8 %all_gather.11 = bf16[32,64,128]{2,1,0:T(8,128)(2,1)S(1)} all-gather(bf16[2,64,128]{2,1,0:T(8,128)(2,1)S(1)} %fusion.12), channel_id=1, replica_groups=mesh['leaf'=16,'col'=2] {'leaf'}, dimensions={0}, use_global_device_ids=true | all-gather | bytes 557056 | tf_op jit(solution)/shard_map/all_gather | solution.py:73
  80.5 0.4 convolution_convert_fusion.2
  80.9 0.1 iota_compare_fusion.3
  81.0 0.1 broadcast_in_dim.59
  81.1 0.1 broadcast_in_dim.60
  81.2 0.0 copy-done.11
  81.2 0.1 eq.28
  81.3 38.7 %all_gather.10 = bf16[32,64,128]{2,1,0:T(8,128)(2,1)S(1)} all-gather(bf16[2,64,128]{2,1,0:T(8,128)(2,1)S(1)} %bitcast.59), channel_id=1, replica_groups=mesh['leaf'=16,'col'=2] {'leaf'}, dimensions={0}, use_global_device_ids=true | all-gather | bytes 557056 | tf_op jit(solution)/shard_map/all_gather | solution.py:72
  119.9 0.4 convolution_convert_fusion.1
  120.4 0.0 copy-done.7
  120.4 0.6 gather_fusion.2
  121.0 0.0 copy-done.10
  121.0 0.1 iota_compare_fusion
  121.1 0.0 copy-done.8
  121.1 0.4 fusion.11
  121.5 0.0 copy-done.5
  121.5 0.4 convolution_bitcast_fusion.1
  121.9 0.1 copy.25
  122.0 0.1 reshape.152
  122.1 0.2 copy.33
  122.3 0.0 collective-permute-done.2
  122.3 0.0 collective-permute-done.3
  122.3 1.0 pad_maximum_fusion.1
  123.3 0.7 gather_fusion.1
  124.0 0.0 copy-done.3
  124.0 1.9 %fusion.9 = f32[16,128,256]{2,1,0:T(8,128)} fusion(bf16[16,64,256]{2,1,0:T(8,128)(2,1)S(1)} %copy-done, f32[16,64,128]{2,1,0:T(8,128)S(1)} %bitcast.57, bf16[16,64,256]{2,1,0:T(8,128)(2,1)S(1)} %copy-done.3, bf16[16,256,128]{2,1,0:T(8,128)(2,1)S(1)} %bitcast.56), kind=kOutput, calls=%fused_computation.15 | convolution fusion | flops 134479872 | bytes 4718592 | tf_op jit(solution)/shard_map/lrk,lrc->lkc/dot_general | solution.py:105
  126.0 0.0 collective-permute-done
  126.0 0.0 collective-permute-done.1
  126.0 1.7 pad_maximum_fusion
  127.6 6.6 %gather_fusion = bf16[128,256,128]{2,1,0:T(8,128)(2,1)} fusion(bf16[32,256,128]{2,1,0:T(8,128)(2,1)S(1)} %bitcast.52, s32[1024]{0:T(1024)S(1)} %pad_clamp_fusion.2), kind=kCustom, calls=%fused_computation | custom fusion | bytes 16777728 | tf_op jit(solution)/shard_map/gather | solution.py:53
  134.2 0.0 copy-start.2
  134.2 12.1 %copy.26 = bf16[128,256,128]{1,2,0:T(8,128)(2,1)} copy(bf16[128,256,128]{2,1,0:T(8,128)(2,1)} %gather_fusion) | data formatting | bytes 16777216 | tf_op jit(solution)/shard_map/gather | solution.py:53
  146.3 0.0 all-gather.2.cloned.1.call-done
  146.3 0.0 copy-done.2
  146.3 12.7 %fusion.4 = f32[16,256,128]{1,2,0:T(8,128)} fusion(f32[16,128,256]{2,1,0:T(8,128)S(1)} %copy-done.2, bf16[16,8,256,256]{3,2,1,0:T(8,128)(2,1)} %all-gather.2.cloned.1.call-done, bf16[16,8,256,128]{2,3,1,0:T(8,128)(2,1)} %bitcast.54, pred[16,8]{1,0:T(8,128)(4,1)S(1)} %iota_compare_fusion), kind=kOutput, calls=%fused_computation.9 | convolution fusion | flops 2152202240 | bytes 29360256 | tf_op jit(solution)/shard_map/lsij,lsjc->lic/dot_general | solution.py:56
  159.0 2.9 %copy.34 = f32[16,256,128]{2,1,0:T(8,128)} copy(f32[16,256,128]{1,2,0:T(8,128)} %fusion.4) | data formatting | bytes 4194304 | tf_op jit(solution)/shard_map/add | solution.py:108
  (11 shorter events, 0.1 us)
Async XLA Ops:
  6.5 1.0 copy-start
  6.5 1.4 copy-start.1
  6.5 139.8 %all-gather.2.cloned.1.call-start = ((), (), s32[]{:S(2)}) async-start(), calls=%async_computation | async-start | bytes 25165824 | tf_op jit(solution)/shard_map/all_gather | solution.py:50
  7.3 14.9 %copy-start.9 = (s32[16,4]{0,1:T(4,128)S(1)}, s32[16,4]{0,1:T(4,128)}, u32[]{:S(2)}) copy-start(s32[16,4]{0,1:T(4,128)} %param.18) | copy-start | bytes 772
  7.3 15.1 %copy-start.4 = (bf16[2,64,512]{2,1,0:T(8,128)(2,1)S(1)}, bf16[2,64,512]{2,1,0:T(8,128)(2,1)}, u32[]{:S(2)}) copy-start(bf16[2,64,512]{2,1,0:T(8,128)(2,1)} %param.19) | copy-start | bytes 393220
  7.3 15.3 %copy-start.6 = (bf16[2,64,64]{2,1,0:T(8,128)(2,1)S(1)}, bf16[2,64,64]{2,1,0:T(8,128)(2,1)}, u32[]{:S(2)}) copy-start(bf16[2,64,64]{2,1,0:T(8,128)(2,1)} %param.22) | copy-start | bytes 49156
  7.3 73.9 %copy-start.11 = (s32[2,4]{1,0:T(2,128)S(1)}, s32[2,4]{1,0:T(2,128)}, u32[]{:S(2)}) copy-start(s32[2,4]{1,0:T(2,128)} %param.21) | copy-start | bytes 100
  7.3 113.1 %copy-start.7 = (bf16[4,64,256]{2,1,0:T(8,128)(2,1)S(1)}, bf16[4,64,256]{2,1,0:T(8,128)(2,1)}, u32[]{:S(2)}) copy-start(bf16[4,64,256]{2,1,0:T(8,128)(2,1)} %param.23) | copy-start | bytes 393220
  7.3 113.7 %copy-start.10 = (s32[16]{0:T(128)S(1)}, s32[16]{0:T(128)}, u32[]{:S(2)}) copy-start(s32[16]{0:T(128)} %param.15) | copy-start | bytes 196
  7.3 113.7 %copy-start.8 = (s32[16,8]{0,1:T(8,128)S(1)}, s32[16,8]{0,1:T(8,128)}, u32[]{:S(2)}) copy-start(s32[16,8]{0,1:T(8,128)} %param.14) | copy-start | bytes 1540
  7.3 114.1 %copy-start.5 = (bf16[2,64,256]{2,1,0:T(8,128)(2,1)S(1)}, bf16[2,64,256]{2,1,0:T(8,128)(2,1)}, u32[]{:S(2)}) copy-start(bf16[2,64,256]{2,1,0:T(8,128)(2,1)} %param.20) | copy-start | bytes 196612
  8.3 114.0 %collective-permute-start.2 = (bf16[8,64,128]{2,1,0:T(8,128)(2,1)S(1)}, bf16[8,64,128]{2,1,0:T(8,128)(2,1)S(1)}, u32[]{:S(2)}, u32[]{:S(2)}) collective-permute-start(bf16[8,64,128]{2,1,0:T(8,128)(2,1)S(1)} %get-tuple-element.7), channel_id=1, source_target_pairs={{0,2},{2,4},{4,6},{6,8},{8,10},{10,12},{12,14},{14,16},{16,18},{18... | collective-permute-start | bytes 393224 | tf_op jit(solution)/shard_map/ppermute | solution.py:17
  13.2 109.1 %collective-permute-start.3 = (bf16[8,64,128]{2,1,0:T(8,128)(2,1)S(1)}, bf16[8,64,128]{2,1,0:T(8,128)(2,1)}, u32[]{:S(2)}, u32[]{:S(2)}) collective-permute-start(bf16[8,64,128]{2,1,0:T(8,128)(2,1)S(1)} %get-tuple-element.8), channel_id=1, source_target_pairs={{2,0},{4,2},{6,4},{8,6},{10,8},{12,10},{14,12},{16,14},{18,16},{20... | collective-permute-start | bytes 393224 | tf_op jit(solution)/shard_map/ppermute | solution.py:18
  15.5 110.4 %collective-permute-start = (bf16[2048,128]{1,0:T(8,128)(2,1)}, bf16[2048,128]{1,0:T(8,128)(2,1)}, u32[]{:S(2)}, u32[]{:S(2)}) collective-permute-start(bf16[2048,128]{1,0:T(8,128)(2,1)} %get-tuple-element.5), channel_id=1, source_target_pairs={{0,2},{2,4},{4,6},{6,8},{8,10},{10,12},{12,14},{14,16},{16,18},{18... | collective-permute-start | bytes 1572872 | tf_op jit(solution)/shard_map/ppermute | solution.py:17
  20.9 105.1 %collective-permute-start.1 = (bf16[2048,128]{1,0:T(8,128)(2,1)}, bf16[2048,128]{1,0:T(8,128)(2,1)}, u32[]{:S(2)}, u32[]{:S(2)}) collective-permute-start(bf16[2048,128]{1,0:T(8,128)(2,1)} %get-tuple-element.6), channel_id=1, source_target_pairs={{2,0},{4,2},{6,4},{8,6},{10,8},{12,10},{14,12},{16,14},{18,16},{20... | collective-permute-start | bytes 1572872 | tf_op jit(solution)/shard_map/ppermute | solution.py:18
  22.7 101.3 %copy-start.3 = (bf16[16,64,256]{2,1,0:T(8,128)(2,1)S(1)}, bf16[16,64,256]{2,1,0:T(8,128)(2,1)}, u32[]{:S(2)}) copy-start(bf16[16,64,256]{2,1,0:T(8,128)(2,1)} %param.17) | copy-start | bytes 1572868
  134.2 12.1 %copy-start.2 = (f32[16,128,256]{2,1,0:T(8,128)S(1)}, f32[16,128,256]{2,1,0:T(8,128)}, u32[]{:S(2)}) copy-start(f32[16,128,256]{2,1,0:T(8,128)} %fusion.9) | copy-start | bytes 6291460
Sparse Core Ops, SparseCore 0:
  8.9 32.7 all-gather.1
where the time goes:
time: 169 us
  blocking collectives  96.5 us (57%)
  local copies, waits for them, and re-layouts  25.4 us (15%)
  matrix products  16.8 us (10%)
  between operations  13.7 us (8%)
  starting transfers between devices  12.8 us (8%)
  other arithmetic  2.82 us (2%)
    all_gather x1, blocking collectives, shards(): lift_piece = lax.all_gather(mid_lift, 'leaf', axis=0, tiled=True)  57.8 us
    all_gather x1, blocking collectives, shards(): coef_piece = lax.all_gather(mid_coef, 'leaf', axis=0, tiled=True)  38.7 us
    gather x2, local copies, waits for them, and re-layouts, shards(): picked = blocks[near_local]  18.7 us
    dot_general x1, matrix products, shards(): jnp.einsum('lsij,lsjc->lic', all_tiles, picked, preferred_element_type=f32)  12.7 us
    ppermute x2, starting transfers between devices, padded(): before = lax.ppermute(last, axis, up)  10.2 us
  transfers between devices with their start and end apart: 5, of which 0 were waited for; matrix products, arithmetic and copies ran while one was open for 17% of the time, Pallas kernels for 0%

commit v1 on v0

--- a/solution.py
+++ b/solution.py
@@ -69,7 +69,21 @@
     parent = (first_mid + jnp.arange(mid_count)) // CHILD
     mid_flat = mid_far.reshape(-1)
     top_range = jnp.arange(total_top)
-    coef_piece = lax.all_gather(mid_coef, "leaf", axis=0, tiled=True)
+    slots = lax.axis_size("leaf")
+    cards = [(s, (s + 1) % slots) for s in range(slots)]
+    pages = [(s, (s - 1) % slots) for s in range(slots)]
+    u1, everything = ([mid_coef], [mid_coef])
+    for _ in range(slots // 2):
+        u1.append(lax.ppermute(u1[-1], "leaf", cards))
+    j0 = 0
+    while j0 < (slots - 1) // 2:
+        everything.append(lax.ppermute(everything[-1], "leaf", pages))
+        j0 += 1
+    coef_piece = jnp.roll(
+        jnp.concatenate([*u1[::-1], *everything[1:]], 0),
+        (lax.axis_index("leaf") - slots // 2) * mid_coef.shape[0],
+        axis=0,
+    )
     lift_piece = lax.all_gather(mid_lift, "leaf", axis=0, tiled=True)
     global_ids = jnp.arange(coef_piece.shape[0])
     group_map = (top_range[:, None] == (global_ids // CHILD)[None, :]).astype(bf16)

time: 169 us -> 175 us (1.036)
  blocking collectives: 96.5 us -> 46.5 us
  starting transfers between devices: 12.8 us -> 51.2 us
  waiting for transfers between devices: 0.72 us -> 16.4 us
    ppermute x0 -> x15, starting transfers between devices: none -> 42 us  [the longest x7 36.8 us: shards(): everything.append(lax.ppermute(everything[-1], 'leaf', pages))]
    all_gather x1 -> x0, blocking collectives: 38.7 us -> none  [shards(): coef_piece = lax.all_gather(mid_coef, 'leaf', axis=0, tiled=True)]
    ppermute x0 -> x15, waiting for transfers between devices: none -> 15.7 us  [the longest x8 11.2 us: shards(): u1.append(lax.ppermute(u1[-1], 'leaf', cards))]
    all_gather x1, blocking collectives: 57.8 us -> 46.5 us  [shards(): lift_piece = lax.all_gather(mid_lift, 'leaf', axis=0, tiled=True)]
    ppermute x2, starting transfers between devices: 10.2 us -> 6.63 us  [padded(): before = lax.ppermute(last, axis, up)]
  transfers between devices with their start and end apart: 5 -> 20, of which waited for: 0 -> 7; matrix products, arithmetic and copies ran while one was open for 17% -> 17% of each run, Pallas kernels for 0% -> 0%
where the time goes in v1:
time: 175 us; the launch traced here: 174 us
  starting transfers between devices  51.2 us (29%)
  blocking collectives  46.5 us (27%)
  local copies, waits for them, and re-layouts  25.8 us (15%)
  matrix products  18.3 us (10%)
  waiting for transfers between devices  16.4 us (9%)
  between operations  13.8 us (8%)
  other arithmetic  1.92 us (1%)
    all_gather x1, blocking collectives, shards(): lift_piece = lax.all_gather(mid_lift, 'leaf', axis=0, tiled=True)  46.5 us
    ppermute x7, starting transfers between devices, shards(): everything.append(lax.ppermute(everything[-1], 'leaf', pages))  36.8 us
    gather x2, local copies, waits for them, and re-layouts, shards(): picked = blocks[near_local]  18.7 us
    dot_general x1, matrix products, shards(): jnp.einsum('lsij,lsjc->lic', all_tiles, picked, preferred_element_type=f32)  12.7 us
    ppermute x8, waiting for transfers between devices, shards(): u1.append(lax.ppermute(u1[-1], 'leaf', cards))  11.2 us
    ppermute x2, starting transfers between devices, padded(): before = lax.ppermute(last, axis, up)  6.63 us
    ppermute x8, starting transfers between devices, shards(): u1.append(lax.ppermute(u1[-1], 'leaf', cards))  5.25 us
    ppermute x7, waiting for transfers between devices, shards(): everything.append(lax.ppermute(everything[-1], 'leaf', pages))  4.48 us
  transfers between devices with their start and end apart: 20, of which 7 were waited for; matrix products, arithmetic and copies ran while one was open for 17% of the time, Pallas kernels for 0%

profile of v1, /device:TPU:0, one launch (start us, length us, event | category | flops | bytes accessed | tf_op | source)
XLA Modules:
  0.0 174.0 jit_solution(17137755611104302989)
XLA Ops:
  6.5 0.7 all-gather.2.cloned.1.call-update
  7.3 0.3 copy-done
  7.6 0.3 copy-done.1
  7.9 0.3 convolution_convert_fusion
  8.3 0.2 convolution_convert_fusion.5
  8.4 3.0 %collective-permute-start.4 = (bf16[2,64,128]{2,1,0:T(8,128)(2,1)S(1)}, bf16[2,64,128]{2,1,0:T(8,128)(2,1)S(1)}, u32[]{:S(2)}, u32[]{:S(2)}) collective-permute-start(bf16[2,64,128]{2,1,0:T(8,128)(2,1)S(1)} %bitcast.61), channel_id=1, source_target_pairs={{0,2},{2,4},{4,6},{6,8},{8,10},{10,12},{12,14},{14,16},{16,18},{18... | collective-permute-start | bytes 98312 | tf_op jit(solution)/shard_map/ppermute | solution.py:77
  11.5 4.1 %collective-permute-start.12 = (bf16[2,64,128]{2,1,0:T(8,128)(2,1)S(1)}, bf16[2,64,128]{2,1,0:T(8,128)(2,1)S(1)}, u32[]{:S(2)}, u32[]{:S(2)}) collective-permute-start(bf16[2,64,128]{2,1,0:T(8,128)(2,1)S(1)} %bitcast.62), channel_id=1, source_target_pairs={{0,30},{2,0},{4,2},{6,4},{8,6},{10,8},{12,10},{14,12},{16,14},{18,... | collective-permute-start | bytes 98312 | tf_op jit(solution)/shard_map/ppermute | solution.py:80
  15.5 1.3 collective-permute-start.2
  16.8 1.3 collective-permute-start.3
  18.1 1.1 fusion.33
  19.2 5.3 %collective-permute-start = (bf16[2048,128]{1,0:T(8,128)(2,1)}, bf16[2048,128]{1,0:T(8,128)(2,1)}, u32[]{:S(2)}, u32[]{:S(2)}) collective-permute-start(bf16[2048,128]{1,0:T(8,128)(2,1)} %get-tuple-element.5), channel_id=1, source_target_pairs={{0,2},{2,4},{4,6},{6,8},{8,10},{10,12},{12,14},{14,16},{16,18},{18... | collective-permute-start | bytes 1572872 | tf_op jit(solution)/shard_map/ppermute | solution.py:17
  24.6 0.1 iota_compare_fusion.3
  24.6 0.1 fusion.12
  24.8 46.5 %all_gather.7 = bf16[32,64,128]{2,1,0:T(8,128)(2,1)S(1)} all-gather(bf16[2,64,128]{2,1,0:T(8,128)(2,1)S(1)} %fusion.12), channel_id=1, replica_groups=mesh['leaf'=16,'col'=2] {'leaf'}, dimensions={0}, use_global_device_ids=true | all-gather | bytes 557056 | tf_op jit(solution)/shard_map/all_gather | solution.py:87
  71.3 0.4 convolution_convert_fusion.2
  71.7 0.1 broadcast_in_dim.59
  71.8 0.1 broadcast_in_dim.60
  71.9 0.6 gather_fusion.2
  72.4 0.0 collective-permute-done.4
  72.4 2.2 %collective-permute-start.5 = (bf16[2,64,128]{2,1,0:T(8,128)(2,1)S(1)}, bf16[2,64,128]{2,1,0:T(8,128)(2,1)S(1)}, u32[]{:S(2)}, u32[]{:S(2)}) collective-permute-start(bf16[2,64,128]{2,1,0:T(8,128)(2,1)S(1)} %collective-permute-done.4), channel_id=1, source_target_pairs={{0,2},{2,4},{4,6},{6,8},{8,10},{10,12},{12,14},{14,16},{16,18},{18... | collective-permute-start | bytes 98312 | tf_op jit(solution)/shard_map/ppermute | solution.py:77
  74.6 1.0 fusion.11
  75.7 4.3 %collective-permute-done.5 = bf16[2,64,128]{2,1,0:T(8,128)(2,1)S(1)} collective-permute-done((bf16[2,64,128]{2,1,0:T(8,128)(2,1)S(1)}, bf16[2,64,128]{2,1,0:T(8,128)(2,1)S(1)}, u32[]{:S(2)}, u32[]{:S(2)}) %collective-permute-start.5) | collective-permute-done | bytes 32800 | tf_op jit(solution)/shard_map/ppermute | solution.py:77
  80.0 0.0 collective-permute-start.6
  80.0 5.7 %collective-permute-start.13 = (bf16[2,64,128]{2,1,0:T(8,128)(2,1)S(1)}, bf16[2,64,128]{2,1,0:T(8,128)(2,1)S(1)}, u32[]{:S(2)}, u32[]{:S(2)}) collective-permute-start(bf16[2,64,128]{2,1,0:T(8,128)(2,1)S(1)} %collective-permute-done.12), channel_id=1, source_target_pairs={{0,30},{2,0},{4,2},{6,4},{8,6},{10,8},{12,10},{14,12},{16,14},{18,... | collective-permute-start | bytes 98312 | tf_op jit(solution)/shard_map/ppermute | solution.py:80
  85.7 1.8 %collective-permute-done.6 = bf16[2,64,128]{2,1,0:T(8,128)(2,1)S(1)} collective-permute-done((bf16[2,64,128]{2,1,0:T(8,128)(2,1)S(1)}, bf16[2,64,128]{2,1,0:T(8,128)(2,1)S(1)}, u32[]{:S(2)}, u32[]{:S(2)}) %collective-permute-start.6) | collective-permute-done | bytes 32800 | tf_op jit(solution)/shard_map/ppermute | solution.py:77
  87.5 0.0 collective-permute-done.13
  87.5 5.7 %collective-permute-start.14 = (bf16[2,64,128]{2,1,0:T(8,128)(2,1)S(1)}, bf16[2,64,128]{2,1,0:T(8,128)(2,1)S(1)}, u32[]{:S(2)}, u32[]{:S(2)}) collective-permute-start(bf16[2,64,128]{2,1,0:T(8,128)(2,1)S(1)} %collective-permute-done.13), channel_id=1, source_target_pairs={{0,30},{2,0},{4,2},{6,4},{8,6},{10,8},{12,10},{14,12},{16,14},{18,... | collective-permute-start | bytes 98312 | tf_op jit(solution)/shard_map/ppermute | solution.py:80
  93.2 1.8 %collective-permute-done.7 = bf16[2,64,128]{2,1,0:T(8,128)(2,1)S(1)} collective-permute-done((bf16[2,64,128]{2,1,0:T(8,128)(2,1)S(1)}, bf16[2,64,128]{2,1,0:T(8,128)(2,1)S(1)}, u32[]{:S(2)}, u32[]{:S(2)}) %collective-permute-start.7) | collective-permute-done | bytes 32800 | tf_op jit(solution)/shard_map/ppermute | solution.py:77
  95.0 0.0 collective-permute-start.8
  95.0 0.1 iota_compare_fusion
  95.1 0.1 copy.27
  95.2 0.1 reshape.160
  95.3 5.7 %collective-permute-start.15 = (bf16[2,64,128]{2,1,0:T(8,128)(2,1)S(1)}, bf16[2,64,128]{2,1,0:T(8,128)(2,1)S(1)}, u32[]{:S(2)}, u32[]{:S(2)}) collective-permute-start(bf16[2,64,128]{2,1,0:T(8,128)(2,1)S(1)} %collective-permute-done.14), channel_id=1, source_target_pairs={{0,30},{2,0},{4,2},{6,4},{8,6},{10,8},{12,10},{14,12},{16,14},{18,... | collective-permute-start | bytes 98312 | tf_op jit(solution)/shard_map/ppermute | solution.py:80
  101.0 1.6 collective-permute-done.8
  102.6 0.1 copy.25
  102.6 0.1 reshape.152
  102.7 0.0 collective-permute-done.15
  102.7 5.8 %collective-permute-start.16 = (bf16[2,64,128]{2,1,0:T(8,128)(2,1)S(1)}, bf16[2,64,128]{2,1,0:T(8,128)(2,1)S(1)}, u32[]{:S(2)}, u32[]{:S(2)}) collective-permute-start(bf16[2,64,128]{2,1,0:T(8,128)(2,1)S(1)} %collective-permute-done.15), channel_id=1, source_target_pairs={{0,30},{2,0},{4,2},{6,4},{8,6},{10,8},{12,10},{14,12},{16,14},{18,... | collective-permute-start | bytes 98312 | tf_op jit(solution)/shard_map/ppermute | solution.py:80
  108.5 1.7 collective-permute-done.9
  110.2 0.1 eq.31
  110.3 0.0 collective-permute-done.2
  110.3 1.3 collective-permute-start.1
  111.6 6.4 %collective-permute-start.17 = (bf16[2,64,128]{2,1,0:T(8,128)(2,1)S(1)}, bf16[2,64,128]{2,1,0:T(8,128)(2,1)S(1)}, u32[]{:S(2)}, u32[]{:S(2)}) collective-permute-start(bf16[2,64,128]{2,1,0:T(8,128)(2,1)S(1)} %collective-permute-done.16), channel_id=1, source_target_pairs={{0,30},{2,0},{4,2},{6,4},{8,6},{10,8},{12,10},{14,12},{16,14},{18,... | collective-permute-start | bytes 98312 | tf_op jit(solution)/shard_map/ppermute | solution.py:80
  118.0 0.0 collective-permute-done.10
  118.0 0.0 collective-permute-start.11
  118.0 0.0 collective-permute-done.3
  118.0 0.1 pad_maximum_fusion.1
  118.1 0.0 copy-start.3
  118.1 0.7 gather_fusion.1
  118.8 3.1 %collective-permute-done.17 = bf16[2,64,128]{2,1,0:T(8,128)(2,1)S(1)} collective-permute-done((bf16[2,64,128]{2,1,0:T(8,128)(2,1)S(1)}, bf16[2,64,128]{2,1,0:T(8,128)(2,1)S(1)}, u32[]{:S(2)}, u32[]{:S(2)}) %collective-permute-start.17) | collective-permute-done | bytes 32800 | tf_op jit(solution)/shard_map/ppermute | solution.py:80
  121.9 3.6 %collective-permute-start.18 = (bf16[2,64,128]{2,1,0:T(8,128)(2,1)S(1)}, bf16[2,64,128]{2,1,0:T(8,128)(2,1)S(1)}, u32[]{:S(2)}, u32[]{:S(2)}) collective-permute-start(bf16[2,64,128]{2,1,0:T(8,128)(2,1)S(1)} %collective-permute-done.17), channel_id=1, source_target_pairs={{0,30},{2,0},{4,2},{6,4},{8,6},{10,8},{12,10},{14,12},{16,14},{18,... | collective-permute-start | bytes 98312 | tf_op jit(solution)/shard_map/ppermute | solution.py:80
  125.5 0.0 collective-permute-done.11
  125.7 1.4 collective-permute-done.18
  127.4 0.4 convolution_convert_fusion.1
  127.8 1.3 convolution_bitcast_fusion.1
  129.1 0.2 copy.33
  129.3 1.9 %fusion.9 = f32[16,128,256]{2,1,0:T(8,128)} fusion(bf16[16,64,256]{2,1,0:T(8,128)(2,1)S(1)} %copy-done, f32[16,64,128]{2,1,0:T(8,128)S(1)} %bitcast.59, bf16[16,64,256]{2,1,0:T(8,128)(2,1)S(1)} %copy-done.3, bf16[16,256,128]{2,1,0:T(8,128)(2,1)S(1)} %bitcast.58), kind=kOutput, calls=%fused_computation.15 | convolution fusion | flops 134479872 | bytes 4718592 | tf_op jit(solution)/shard_map/lrk,lrc->lkc/dot_general | solution.py:119
  131.2 0.0 collective-permute-done
  131.2 0.0 collective-permute-done.1
  131.2 1.7 pad_maximum_fusion
  132.9 6.6 %gather_fusion = bf16[128,256,128]{2,1,0:T(8,128)(2,1)} fusion(bf16[32,256,128]{2,1,0:T(8,128)(2,1)S(1)} %bitcast.54, s32[1024]{0:T(1024)S(1)} %pad_clamp_fusion.2), kind=kCustom, calls=%fused_computation | custom fusion | bytes 16777728 | tf_op jit(solution)/shard_map/gather | solution.py:53
  139.5 12.1 %copy.26 = bf16[128,256,128]{1,2,0:T(8,128)(2,1)} copy(bf16[128,256,128]{2,1,0:T(8,128)(2,1)} %gather_fusion) | data formatting | bytes 16777216 | tf_op jit(solution)/shard_map/gather | solution.py:53
  151.6 12.7 %fusion.4 = f32[16,256,128]{1,2,0:T(8,128)} fusion(f32[16,128,256]{2,1,0:T(8,128)S(1)} %copy-done.2, bf16[16,8,256,256]{3,2,1,0:T(8,128)(2,1)} %all-gather.2.cloned.1.call-done, bf16[16,8,256,128]{2,3,1,0:T(8,128)(2,1)} %bitcast.56, pred[16,8]{1,0:T(8,128)(4,1)S(1)} %iota_compare_fusion), kind=kOutput, calls=%fused_computation.9 | convolution fusion | flops 2152202240 | bytes 29360256 | tf_op jit(solution)/shard_map/lsij,lsjc->lic/dot_general | solution.py:56
  164.3 2.9 %copy.34 = f32[16,256,128]{2,1,0:T(8,128)} copy(f32[16,256,128]{1,2,0:T(8,128)} %fusion.4) | data formatting | bytes 4194304 | tf_op jit(solution)/shard_map/add | solution.py:122
  (71 shorter events, 0.6 us)
Async XLA Ops:
  6.5 1.0 copy-start
  6.5 1.4 copy-start.1
  6.5 1.7 copy-start.4
  6.5 145.1 %all-gather.2.cloned.1.call-start = ((), (), s32[]{:S(2)}) async-start(), calls=%async_computation | async-start | bytes 25165824 | tf_op jit(solution)/shard_map/all_gather | solution.py:50
  7.3 17.4 %copy-start.5 = (bf16[2,64,64]{2,1,0:T(8,128)(2,1)S(1)}, bf16[2,64,64]{2,1,0:T(8,128)(2,1)}, u32[]{:S(2)}) copy-start(bf16[2,64,64]{2,1,0:T(8,128)(2,1)} %param.22) | copy-start | bytes 49156
  7.3 64.6 %copy-start.6 = (bf16[4,64,256]{2,1,0:T(8,128)(2,1)S(1)}, bf16[4,64,256]{2,1,0:T(8,128)(2,1)}, u32[]{:S(2)}) copy-start(bf16[4,64,256]{2,1,0:T(8,128)(2,1)} %param.23) | copy-start | bytes 393220
  7.3 72.7 %copy-start.7 = (s32[16,8]{0,1:T(8,128)S(1)}, s32[16,8]{0,1:T(8,128)}, u32[]{:S(2)}) copy-start(s32[16,8]{0,1:T(8,128)} %param.14) | copy-start | bytes 1540
  7.3 80.2 %copy-start.8 = (s32[16,4]{0,1:T(4,128)S(1)}, s32[16,4]{0,1:T(4,128)}, u32[]{:S(2)}) copy-start(s32[16,4]{0,1:T(4,128)} %param.18) | copy-start | bytes 772
  7.3 87.7 %copy-start.9 = (s32[16]{0:T(128)S(1)}, s32[16]{0:T(128)}, u32[]{:S(2)}) copy-start(s32[16]{0:T(128)} %param.15) | copy-start | bytes 196
  7.3 102.9 %copy-start.10 = (s32[2,4]{1,0:T(2,128)S(1)}, s32[2,4]{1,0:T(2,128)}, u32[]{:S(2)}) copy-start(s32[2,4]{1,0:T(2,128)} %param.21) | copy-start | bytes 100
  8.4 64.0 %collective-permute-start.4 = (bf16[2,64,128]{2,1,0:T(8,128)(2,1)S(1)}, bf16[2,64,128]{2,1,0:T(8,128)(2,1)S(1)}, u32[]{:S(2)}, u32[]{:S(2)}) collective-permute-start(bf16[2,64,128]{2,1,0:T(8,128)(2,1)S(1)} %bitcast.61), channel_id=1, source_target_pairs={{0,2},{2,4},{4,6},{6,8},{8,10},{10,12},{12,14},{14,16},{16,18},{18... | collective-permute-start | bytes 98312 | tf_op jit(solution)/shard_map/ppermute | solution.py:77
  11.5 68.6 %collective-permute-start.12 = (bf16[2,64,128]{2,1,0:T(8,128)(2,1)S(1)}, bf16[2,64,128]{2,1,0:T(8,128)(2,1)S(1)}, u32[]{:S(2)}, u32[]{:S(2)}) collective-permute-start(bf16[2,64,128]{2,1,0:T(8,128)(2,1)S(1)} %bitcast.62), channel_id=1, source_target_pairs={{0,30},{2,0},{4,2},{6,4},{8,6},{10,8},{12,10},{14,12},{16,14},{18,... | collective-permute-start | bytes 98312 | tf_op jit(solution)/shard_map/ppermute | solution.py:80
  15.5 94.7 %collective-permute-start.2 = (bf16[8,64,128]{2,1,0:T(8,128)(2,1)S(1)}, bf16[8,64,128]{2,1,0:T(8,128)(2,1)S(1)}, u32[]{:S(2)}, u32[]{:S(2)}) collective-permute-start(bf16[8,64,128]{2,1,0:T(8,128)(2,1)S(1)} %get-tuple-element.7), channel_id=1, source_target_pairs={{0,2},{2,4},{4,6},{6,8},{8,10},{10,12},{12,14},{14,16},{16,18},{18... | collective-permute-start | bytes 393224 | tf_op jit(solution)/shard_map/ppermute | solution.py:17
  16.8 101.1 %collective-permute-start.3 = (bf16[8,64,128]{2,1,0:T(8,128)(2,1)S(1)}, bf16[8,64,128]{2,1,0:T(8,128)(2,1)S(1)}, u32[]{:S(2)}, u32[]{:S(2)}) collective-permute-start(bf16[8,64,128]{2,1,0:T(8,128)(2,1)S(1)} %get-tuple-element.8), channel_id=1, source_target_pairs={{2,0},{4,2},{6,4},{8,6},{10,8},{12,10},{14,12},{16,14},{18,16},{20... | collective-permute-start | bytes 393224 | tf_op jit(solution)/shard_map/ppermute | solution.py:18
  19.2 112.0 %collective-permute-start = (bf16[2048,128]{1,0:T(8,128)(2,1)}, bf16[2048,128]{1,0:T(8,128)(2,1)}, u32[]{:S(2)}, u32[]{:S(2)}) collective-permute-start(bf16[2048,128]{1,0:T(8,128)(2,1)} %get-tuple-element.5), channel_id=1, source_target_pairs={{0,2},{2,4},{4,6},{6,8},{8,10},{10,12},{12,14},{14,16},{16,18},{18... | collective-permute-start | bytes 1572872 | tf_op jit(solution)/shard_map/ppermute | solution.py:17
  72.4 7.6 %collective-permute-start.5 = (bf16[2,64,128]{2,1,0:T(8,128)(2,1)S(1)}, bf16[2,64,128]{2,1,0:T(8,128)(2,1)S(1)}, u32[]{:S(2)}, u32[]{:S(2)}) collective-permute-start(bf16[2,64,128]{2,1,0:T(8,128)(2,1)S(1)} %collective-permute-done.4), channel_id=1, source_target_pairs={{0,2},{2,4},{4,6},{6,8},{8,10},{10,12},{12,14},{14,16},{16,18},{18... | collective-permute-start | bytes 98312 | tf_op jit(solution)/shard_map/ppermute | solution.py:77
  80.0 7.5 %collective-permute-start.6 = (bf16[2,64,128]{2,1,0:T(8,128)(2,1)S(1)}, bf16[2,64,128]{2,1,0:T(8,128)(2,1)S(1)}, u32[]{:S(2)}, u32[]{:S(2)}) collective-permute-start(bf16[2,64,128]{2,1,0:T(8,128)(2,1)S(1)} %collective-permute-done.5), channel_id=1, source_target_pairs={{0,2},{2,4},{4,6},{6,8},{8,10},{10,12},{12,14},{14,16},{16,18},{18... | collective-permute-start | bytes 98312 | tf_op jit(solution)/shard_map/ppermute | solution.py:77
  80.0 7.5 %collective-permute-start.13 = (bf16[2,64,128]{2,1,0:T(8,128)(2,1)S(1)}, bf16[2,64,128]{2,1,0:T(8,128)(2,1)S(1)}, u32[]{:S(2)}, u32[]{:S(2)}) collective-permute-start(bf16[2,64,128]{2,1,0:T(8,128)(2,1)S(1)} %collective-permute-done.12), channel_id=1, source_target_pairs={{0,30},{2,0},{4,2},{6,4},{8,6},{10,8},{12,10},{14,12},{16,14},{18,... | collective-permute-start | bytes 98312 | tf_op jit(solution)/shard_map/ppermute | solution.py:80
  87.5 7.5 %collective-permute-start.7 = (bf16[2,64,128]{2,1,0:T(8,128)(2,1)S(1)}, bf16[2,64,128]{2,1,0:T(8,128)(2,1)S(1)}, u32[]{:S(2)}, u32[]{:S(2)}) collective-permute-start(bf16[2,64,128]{2,1,0:T(8,128)(2,1)S(1)} %collective-permute-done.6), channel_id=1, source_target_pairs={{0,2},{2,4},{4,6},{6,8},{8,10},{10,12},{12,14},{14,16},{16,18},{18... | collective-permute-start | bytes 98312 | tf_op jit(solution)/shard_map/ppermute | solution.py:77
  87.5 7.8 %collective-permute-start.14 = (bf16[2,64,128]{2,1,0:T(8,128)(2,1)S(1)}, bf16[2,64,128]{2,1,0:T(8,128)(2,1)S(1)}, u32[]{:S(2)}, u32[]{:S(2)}) collective-permute-start(bf16[2,64,128]{2,1,0:T(8,128)(2,1)S(1)} %collective-permute-done.13), channel_id=1, source_target_pairs={{0,30},{2,0},{4,2},{6,4},{8,6},{10,8},{12,10},{14,12},{16,14},{18,... | collective-permute-start | bytes 98312 | tf_op jit(solution)/shard_map/ppermute | solution.py:80
  95.0 7.5 %collective-permute-start.8 = (bf16[2,64,128]{2,1,0:T(8,128)(2,1)S(1)}, bf16[2,64,128]{2,1,0:T(8,128)(2,1)S(1)}, u32[]{:S(2)}, u32[]{:S(2)}) collective-permute-start(bf16[2,64,128]{2,1,0:T(8,128)(2,1)S(1)} %collective-permute-done.7), channel_id=1, source_target_pairs={{0,2},{2,4},{4,6},{6,8},{8,10},{10,12},{12,14},{14,16},{16,18},{18... | collective-permute-start | bytes 98312 | tf_op jit(solution)/shard_map/ppermute | solution.py:77
  95.3 7.4 %collective-permute-start.15 = (bf16[2,64,128]{2,1,0:T(8,128)(2,1)S(1)}, bf16[2,64,128]{2,1,0:T(8,128)(2,1)S(1)}, u32[]{:S(2)}, u32[]{:S(2)}) collective-permute-start(bf16[2,64,128]{2,1,0:T(8,128)(2,1)S(1)} %collective-permute-done.14), channel_id=1, source_target_pairs={{0,30},{2,0},{4,2},{6,4},{8,6},{10,8},{12,10},{14,12},{16,14},{18,... | collective-permute-start | bytes 98312 | tf_op jit(solution)/shard_map/ppermute | solution.py:80
  102.5 7.6 %collective-permute-start.9 = (bf16[2,64,128]{2,1,0:T(8,128)(2,1)S(1)}, bf16[2,64,128]{2,1,0:T(8,128)(2,1)S(1)}, u32[]{:S(2)}, u32[]{:S(2)}) collective-permute-start(bf16[2,64,128]{2,1,0:T(8,128)(2,1)S(1)} %collective-permute-done.8), channel_id=1, source_target_pairs={{0,2},{2,4},{4,6},{6,8},{8,10},{10,12},{12,14},{14,16},{16,18},{18... | collective-permute-start | bytes 98312 | tf_op jit(solution)/shard_map/ppermute | solution.py:77
  102.7 8.8 %collective-permute-start.16 = (bf16[2,64,128]{2,1,0:T(8,128)(2,1)S(1)}, bf16[2,64,128]{2,1,0:T(8,128)(2,1)S(1)}, u32[]{:S(2)}, u32[]{:S(2)}) collective-permute-start(bf16[2,64,128]{2,1,0:T(8,128)(2,1)S(1)} %collective-permute-done.15), channel_id=1, source_target_pairs={{0,30},{2,0},{4,2},{6,4},{8,6},{10,8},{12,10},{14,12},{16,14},{18,... | collective-permute-start | bytes 98312 | tf_op jit(solution)/shard_map/ppermute | solution.py:80
  110.2 7.8 %collective-permute-start.10 = (bf16[2,64,128]{2,1,0:T(8,128)(2,1)S(1)}, bf16[2,64,128]{2,1,0:T(8,128)(2,1)S(1)}, u32[]{:S(2)}, u32[]{:S(2)}) collective-permute-start(bf16[2,64,128]{2,1,0:T(8,128)(2,1)S(1)} %collective-permute-done.9), channel_id=1, source_target_pairs={{0,2},{2,4},{4,6},{6,8},{8,10},{10,12},{12,14},{14,16},{16,18},{18... | collective-permute-start | bytes 98312 | tf_op jit(solution)/shard_map/ppermute | solution.py:77
  110.3 21.0 %collective-permute-start.1 = (bf16[2048,128]{1,0:T(8,128)(2,1)}, bf16[2048,128]{1,0:T(8,128)(2,1)}, u32[]{:S(2)}, u32[]{:S(2)}) collective-permute-start(bf16[2048,128]{1,0:T(8,128)(2,1)} %get-tuple-element.6), channel_id=1, source_target_pairs={{2,0},{4,2},{6,4},{8,6},{10,8},{12,10},{14,12},{16,14},{18,16},{20... | collective-permute-start | bytes 1572872 | tf_op jit(solution)/shard_map/ppermute | solution.py:18
  111.6 10.3 %collective-permute-start.17 = (bf16[2,64,128]{2,1,0:T(8,128)(2,1)S(1)}, bf16[2,64,128]{2,1,0:T(8,128)(2,1)S(1)}, u32[]{:S(2)}, u32[]{:S(2)}) collective-permute-start(bf16[2,64,128]{2,1,0:T(8,128)(2,1)S(1)} %collective-permute-done.16), channel_id=1, source_target_pairs={{0,30},{2,0},{4,2},{6,4},{8,6},{10,8},{12,10},{14,12},{16,14},{18,... | collective-permute-start | bytes 98312 | tf_op jit(solution)/shard_map/ppermute | solution.py:80
  118.0 7.5 %collective-permute-start.11 = (bf16[2,64,128]{2,1,0:T(8,128)(2,1)S(1)}, bf16[2,64,128]{2,1,0:T(8,128)(2,1)S(1)}, u32[]{:S(2)}, u32[]{:S(2)}) collective-permute-start(bf16[2,64,128]{2,1,0:T(8,128)(2,1)S(1)} %collective-permute-done.10), channel_id=1, source_target_pairs={{0,2},{2,4},{4,6},{6,8},{8,10},{10,12},{12,14},{14,16},{16,18},{18... | collective-permute-start | bytes 98312 | tf_op jit(solution)/shard_map/ppermute | solution.py:77
  118.1 11.2 %copy-start.3 = (bf16[16,64,256]{2,1,0:T(8,128)(2,1)S(1)}, bf16[16,64,256]{2,1,0:T(8,128)(2,1)}, u32[]{:S(2)}) copy-start(bf16[16,64,256]{2,1,0:T(8,128)(2,1)} %param.17) | copy-start | bytes 1572868
  121.9 5.2 %collective-permute-start.18 = (bf16[2,64,128]{2,1,0:T(8,128)(2,1)S(1)}, bf16[2,64,128]{2,1,0:T(8,128)(2,1)S(1)}, u32[]{:S(2)}, u32[]{:S(2)}) collective-permute-start(bf16[2,64,128]{2,1,0:T(8,128)(2,1)S(1)} %collective-permute-done.17), channel_id=1, source_target_pairs={{0,30},{2,0},{4,2},{6,4},{8,6},{10,8},{12,10},{14,12},{16,14},{18,... | collective-permute-start | bytes 98312 | tf_op jit(solution)/shard_map/ppermute | solution.py:80
  139.5 12.1 %copy-start.2 = (f32[16,128,256]{2,1,0:T(8,128)S(1)}, f32[16,128,256]{2,1,0:T(8,128)}, u32[]{:S(2)}) copy-start(f32[16,128,256]{2,1,0:T(8,128)} %fusion.9) | copy-start | bytes 6291460
Sparse Core Ops, SparseCore 0:
  8.9 32.7 all-gather.1
